TPU v7x, 32 devices: a whole 2x2x4 slice. The times are simulated.
32 devices in a mesh: shot: 2 (over core), probe: 16 (over z, y, x).
Axes of the slice: x: 2, y: 2, z: 4, core: 2. Of those that a mesh axis runs over, the one named last changes fastest.
Arguments:
- probes: float32 [32, 256, 512], P('probe'), may hold values from -6 to 6
- coarse_sample: float32 [32, 256, 512], P('probe', 'shot'), may hold values from -6 to 6
- coefficient: float32 [256, 512], replicated, may hold values from 0.05 to 0.45
- receiver: float32 [256, 512], replicated, may hold values from 0.05 to 0.5
- checkpoints: float32 [4, 2, 256, 512], P('shot', None, 'probe'), may hold values from -6 to 6
- encodings: int32 [4, 256], P('shot'), may hold values from -1 to 1, as said below
- wavelet: float32 [3, 256], replicated, may hold values from -6 to 6
- bounds: int32 [33], replicated, may hold values from 0 to 256, as said below
Outputs:
- samples: float32 [32, 256, 512], P('probe', 'shot')
Inputs may be any that keep to these rules, and one draw needn't show every extreme that they name: `encodings`: every entry is -1 or 1. bounds[0] = 0 and bounds[32] = 256; the entries rise strictly; blocks 2 i and 2 i + 1 together hold exactly 16 rows.
All inputs are finite; a program needn't handle non-finite values.
Results may differ from a plain program's by a relative error of at most 0.000094.
Values sent between devices are 32-bit elements; how exact they have to be, the bound alone decides.
A program may use at most 128 MiB of HBM per device.

v0:
```python
import jax
import jax.numpy as jnp
from jax import lax
from jax.sharding import PartitionSpec as P

NZ = 512
NSHOT = 256
NT = 4


def laplace(values):
    pad_width = [(0, 0)] * (values.ndim - 2) + [(1, 1), (1, 1)]
    padded = jnp.pad(values, pad_width)
    return (
        padded[..., 2:, 1:-1]
        + padded[..., :-2, 1:-1]
        + padded[..., 1:-1, 2:]
        + padded[..., 1:-1, :-2]
        - 4.0 * values
    )


def shot_sources(encodings, wavelet):
    columns = jnp.arange(NZ)
    spacing = NZ // NSHOT
    position = jnp.arange(NSHOT) * NZ // NSHOT + spacing // 2
    onehot = (position[:, None] == columns[None, :]).astype(jnp.float32)
    amplitude = encodings.astype(jnp.float32)[:, None, :] * wavelet[None, :, :]
    return jnp.einsum("stk,kz->stz", amplitude, onehot, precision=lax.Precision.HIGHEST)


def block_parity(row_index, bounds):
    inner = bounds[1:-1]
    return jnp.sum((row_index[:, None] >= inner[None, :]).astype(jnp.int32), axis=1) % 2


def hessian_term(vectors, levels, coefficient, weight_square):
    before = jnp.zeros_like(vectors)
    current = jnp.zeros_like(vectors)
    deltas = []
    for moment in range(NT):
        following = (
            2.0 * current - before + coefficient * laplace(current) + vectors * levels[moment]
        )
        before, current = (current, following)
        deltas.append(following)
    upcoming = jnp.zeros_like(vectors)
    beyond = jnp.zeros_like(vectors)
    gradient = jnp.zeros_like(vectors)
    for moment in range(NT, 0, -1):
        adjoint = (
            weight_square * deltas[moment - 1]
            + 2.0 * upcoming
            + laplace(coefficient * upcoming)
            - beyond
        )
        gradient = gradient + levels[moment - 1] * adjoint
        beyond, upcoming = (upcoming, adjoint)
    return gradient


def on_device(
    probes, coarse_sample, coefficient, receiver, checkpoints, encodings, wavelet, bounds
):
    num_rows = probes.shape[1]
    source_at = num_rows // 2
    sources = shot_sources(encodings, wavelet)
    colour = jnp.arange(probes.shape[0]) % 2
    parity_all = block_parity(jnp.arange(num_rows), bounds)
    support = (parity_all[None, :] == colour[:, None]).astype(jnp.float32)
    vectors = probes * support[:, :, None]
    weight_square = receiver * receiver
    accumulated = jnp.zeros_like(probes)
    for member in range(checkpoints.shape[0]):
        stored = lax.all_gather(checkpoints[member], "probe", axis=1, tiled=True)
        at_source = (jnp.arange(num_rows) == source_at).astype(jnp.float32)[:, None]
        before = stored[0]
        current = stored[1]
        history = [current]
        for moment in range(NT - 1):
            following = (
                2.0 * current
                - before
                + coefficient * laplace(current)
                + at_source * sources[member, moment][None, :]
            )
            before, current = (current, following)
            history.append(current)
        levels = jnp.stack(history)
        accumulated = accumulated + hessian_term(vectors, levels, coefficient, weight_square)
    out_rows = coarse_sample.shape[1]
    summed = lax.psum(accumulated, "shot")
    share = lax.dynamic_slice_in_dim(summed, lax.axis_index("shot") * out_rows, out_rows, 1)
    row_out = lax.axis_index("shot") * out_rows + jnp.arange(out_rows)
    keep = (block_parity(row_out, bounds)[None, :] != colour[:, None]).astype(jnp.float32)
    return keep[:, :, None] * (share - coarse_sample)


def solution(mesh):
    return jax.shard_map(
        on_device,
        mesh=mesh,
        in_specs=(
            P("probe", None, None),
            P("probe", "shot", None),
            P(),
            P(),
            P("shot", None, "probe", None),
            P("shot", None),
            P(),
            P(),
        ),
        out_specs=P("probe", "shot", None),
        check_vma=False,
    )
```

profile of v0, /device:TPU:1, one launch (start us, length us, event | category | flops | bytes accessed | tf_op | source)
XLA Modules:
  0.0 185.9 jit_solution(16880601217154744731)
XLA Ops:
  6.5 1.5 fusion.153
  8.1 0.0 all-gather.7.cloned.1.call-update
  8.1 0.0 all-gather.5.cloned.1.call-start
  8.1 0.7 all-gather.5.cloned.1.call-update
  8.8 0.0 all-reduce.22.cloned.1.call-start
  8.9 0.7 convert_element_type.69
  9.6 0.7 slice.296
  10.3 1.4 mul.554
  11.7 0.1 convert_reduce_fusion
  11.8 0.1 compare_convert_fusion
  11.9 0.3 fusion.138
  12.2 0.0 copy-start
  12.3 53.7 %all-gather.7.cloned.1.call-done = f32[1,2,256,512]{3,2,1,0:T(8,128)} async-done(((f32[1,2,16,512]{3,2,1,0:T(8,128)}), f32[1,2,256,512]{3,2,1,0:T(8,128)}) %all-gather.7.cloned.1.call-update) | async-done | bytes 1048592 | tf_op jit(solution)/shard_map/all_gather | solution.py:75
  65.9 1.2 slice_bitcast_fusion.1
  67.1 0.0 copy-start.7
  67.1 55.8 %all-gather.5.cloned.1.call-done = f32[1,2,256,512]{3,2,1,0:T(8,128)} async-done(((f32[1,2,16,512]{3,2,1,0:T(8,128)}), f32[1,2,256,512]{3,2,1,0:T(8,128)}) %all-gather.5.cloned.1.call-update) | async-done | bytes 1048592 | tf_op jit(solution)/shard_map/all_gather | solution.py:75
  122.9 1.1 slice_bitcast_fusion.3
  124.0 0.0 copy-start.9
  124.0 0.0 copy-done
  124.0 0.0 copy-done.20
  124.0 0.0 copy-start.21
  124.0 1.9 %fusion.116 = (f32[256,512]{1,0:T(8,128)S(1)}, f32[256,512]{1,0:T(8,128)S(1)}) fusion(f32[256,512]{1,0:T(8,128)S(1)} %copy-done, f32[256,512]{1,0:T(8,128)S(1)} %slice_bitcast_fusion.1, f32[1,2,256,512]{3,2,1,0:T(8,128)S(1)} %copy-done.20, f32[512]{0:T(512)S(1)} %bitcast.33, f32[256]{0:T(256)S(1)} %compare_convert_fusion.1, f32[512]{0:T(512)S(1)} %bitcast.34, ...), kind=kLoop, calls=%fused_computation.198 | loop fusion | flops 2883584 | bytes 3675136 | tf_op jit(solution)/shard_map/add | solution.py:82
  126.0 0.0 copy-start.2
  126.0 0.0 copy-done.21
  126.0 0.8 fusion.123
  126.9 0.0 copy-start.11
  126.9 0.1 broadcast.253
  126.9 0.0 copy-start.1
  126.9 1.1 fusion.130
  128.1 0.4 copy-done.1
  128.5 0.3 multiply_add_fusion
  128.8 0.8 fusion.49
  129.6 0.0 copy-done.11
  129.6 1.5 fusion.56
  131.1 0.9 fusion.13
  132.0 0.3 fusion.109
  132.4 3.2 %broadcast_multiply_fusion.2 = (f32[2,256,512]{2,1,0:T(8,128)S(1)}, f32[2,256,512]{2,1,0:T(8,128)S(1)}, f32[2,256,512]{2,1,0:T(8,128)}, f32[2,256,512]{2,1,0:T(8,128)S(1)}) fusion(f32[256,512]{1,0:T(8,128)S(1)} %copy-done, f32[256,512]{1,0:T(8,128)S(1)} %fusion.109, f32[256,512]{1,0:T(8,128)S(1)} %get-tuple-element.25, f32[2,256,512]{2,1,0:T(8,128)S(1)} %copy-done.1, ...), kind=kLoop, calls=%fused_computation.226 | loop fusion | flops 7602176 | bytes 12060672 | tf_op jit(solution)/shard_map/mul | solution.py:54
  135.6 2.2 %broadcast_multiply_fusion.1 = (f32[2,256,512]{2,1,0:T(8,128)}, f32[2,256,512]{2,1,0:T(8,128)}) fusion(f32[256,512]{1,0:T(8,128)S(1)} %copy-done, f32[2,256,512]{2,1,0:T(8,128)S(1)} %get-tuple-element.9, f32[2,256,512]{2,1,0:T(8,128)S(1)} %get-tuple-element.10, f32[2,256,512]{2,1,0:T(8,128)S(1)} %get-tuple-element.19, f32[256,512]{1,0:T(8,128)S(1)} %mul.554), kind=kLoop, calls=%fused_computation.225 | loop fusion | flops 2621440 | bytes 6291456 | tf_op jit(solution)/shard_map/mul | solution.py:54
  137.8 9.3 %broadcast_multiply_fusion = (f32[2,256,512]{2,1,0:T(8,128)}, f32[2,256,512]{2,1,0:T(8,128)}, f32[2,256,512]{2,1,0:T(8,128)}, f32[2,256,512]{2,1,0:T(8,128)}) fusion(f32[256,512]{1,0:T(8,128)S(1)} %copy-done, f32[2,256,512]{2,1,0:T(8,128)S(1)} %get-tuple-element.10, f32[2,256,512]{2,1,0:T(8,128)} %get-tuple-element.7, f32[2,256,512]{2,1,0:T(8,128)} %get-tuple-element.8, ...), kind=kLoop, calls=%fused_computation.224 | loop fusion | flops 5505024 | bytes 12582912 | tf_op jit(solution)/shard_map/mul | solution.py:54
  147.2 0.0 copy-start.12
  147.2 4.6 %broadcast_multiply_fusion.3 = (f32[2,256,512]{2,1,0:T(8,128)S(1)}, f32[2,256,512]{2,1,0:T(8,128)S(1)}) fusion(f32[256,512]{1,0:T(8,128)S(1)} %copy-done, f32[2,256,512]{2,1,0:T(8,128)S(1)} %get-tuple-element.18, f32[2,256,512]{2,1,0:T(8,128)} %get-tuple-element.23, f32[2,256,512]{2,1,0:T(8,128)} %get-tuple-element.24, ...), kind=kLoop, calls=%fused_computation.227 | loop fusion | flops 2883584 | bytes 7340032 | tf_op jit(solution)/shard_map/mul | solution.py:54
  151.9 0.0 copy-done.19
  152.0 4.9 %fusion.42 = f32[2,256,512]{2,1,0:T(8,128)} fusion(f32[2,256,512]{2,1,0:T(8,128)S(1)} %copy-done.4, f32[2,256,512]{2,1,0:T(8,128)S(1)} %get-tuple-element.11, f32[2,256,512]{2,1,0:T(8,128)S(1)} %copy-done.6, f32[2,256,512]{2,1,0:T(8,128)S(1)} %copy-done.19, f32[2,256,512]{2,1,0:T(8,128)} %get-tuple-element.6, f32[2,256,512]{2,1,0:T(8,128)S(1)} %get-tuple-element.21, ...), kind=kLoop, calls=%fused_computation.94 | loop fusion | flops 9175040 | bytes 16252928 | tf_op jit(solution)/shard_map/add | solution.py:90
  156.9 0.0 all-reduce.22.cloned.1.call-update
  157.0 0.1 convert_reduce_fusion.1
  157.1 0.1 compare_convert_fusion.2
  157.1 20.2 %all-reduce.22.cloned.1.call-done = f32[2,256,512]{2,1,0:T(8,128)} async-done(((f32[2,256,512]{2,1,0:T(8,128)}), f32[2,256,512]{2,1,0:T(8,128)}) %all-reduce.22.cloned.1.call-update) | async-done | bytes 1048592 | tf_op jit(solution)/shard_map/psum | solution.py:92
  177.4 1.9 %subtract_multiply_fusion = f32[2,128,512]{2,1,0:T(8,128)} fusion(f32[2,128,512]{2,1,0:T(8,128)S(1)} %copy-done.22, f32[2,256,512]{2,1,0:T(8,128)} %all-reduce.22.cloned.1.call-done, s32[]{:T(128)S(6)} %select_n.49, f32[2,128]{1,0:T(2,128)S(1)} %compare_convert_fusion.2), kind=kLoop, calls=%fused_computation.223 | loop fusion | flops 262144 | bytes 1573892 | tf_op jit(solution)/shard_map/mul | solution.py:96
  (42 shorter events, 0.1 us)
Async XLA Ops:
  6.5 5.4 %copy-start.23 = (f32[3,256]{1,0:T(4,128)S(1)}, f32[3,256]{1,0:T(4,128)}, u32[]{:S(2)}) copy-start(f32[3,256]{1,0:T(4,128)} %param.14) | copy-start | bytes 9220
  6.5 59.4 %all-gather.7.cloned.1.call-start = ((), (), s32[]{:S(2)}) async-start(), calls=%async_computation.2 | async-start | bytes 1114112 | tf_op jit(solution)/shard_map/all_gather | solution.py:75
  8.1 114.8 %all-gather.5.cloned.1.call-start = ((), (), s32[]{:S(2)}) async-start(), calls=%async_computation.1 | async-start | bytes 1114112 | tf_op jit(solution)/shard_map/all_gather | solution.py:75
  8.8 168.6 %all-reduce.22.cloned.1.call-start = ((), (), s32[]{:S(2)}) async-start(), calls=%async_computation | async-start | bytes 2097152 | tf_op jit(solution)/shard_map/psum | solution.py:92
  12.2 111.8 %copy-start = (f32[256,512]{1,0:T(8,128)S(1)}, f32[256,512]{1,0:T(8,128)}, u32[]{:S(2)}) copy-start(f32[256,512]{1,0:T(8,128)} %param.10) | copy-start | bytes 1572868
  65.9 58.1 %copy-start.20 = (f32[1,2,256,512]{3,2,1,0:T(8,128)S(1)}, f32[1,2,256,512]{3,2,1,0:T(8,128)}, u32[]{:S(2)}) copy-start(f32[1,2,256,512]{3,2,1,0:T(8,128)} %all-gather.7.cloned.1.call-done) | copy-start | bytes 3145732
  67.1 61.0 %copy-start.7 = (f32[256,512]{1,0:T(8,128)}, f32[256,512]{1,0:T(8,128)S(1)}, u32[]{:S(2)}) copy-start(f32[256,512]{1,0:T(8,128)S(1)} %slice_bitcast_fusion.1) | copy-start | bytes 1572868
  124.0 4.1 %copy-start.9 = (f32[256,512]{1,0:T(8,128)}, f32[256,512]{1,0:T(8,128)S(1)}, u32[]{:S(2)}) copy-start(f32[256,512]{1,0:T(8,128)S(1)} %slice_bitcast_fusion.3) | copy-start | bytes 1572868
  124.0 2.0 %copy-start.21 = (f32[1,2,256,512]{3,2,1,0:T(8,128)S(1)}, f32[1,2,256,512]{3,2,1,0:T(8,128)}, u32[]{:S(2)}) copy-start(f32[1,2,256,512]{3,2,1,0:T(8,128)} %all-gather.5.cloned.1.call-done) | copy-start | bytes 3145732
  126.0 2.8 %copy-start.2 = (f32[256,512]{1,0:T(8,128)}, f32[256,512]{1,0:T(8,128)S(1)}, u32[]{:S(2)}) copy-start(f32[256,512]{1,0:T(8,128)S(1)} %get-tuple-element.29) | copy-start | bytes 1572868
  126.9 2.7 %copy-start.11 = (f32[256,512]{1,0:T(8,128)}, f32[256,512]{1,0:T(8,128)S(1)}, u32[]{:S(2)}) copy-start(f32[256,512]{1,0:T(8,128)S(1)} %get-tuple-element.27) | copy-start | bytes 1572868
  126.9 4.2 %copy-start.13 = (f32[256,512]{1,0:T(8,128)}, f32[256,512]{1,0:T(8,128)S(1)}, u32[]{:S(2)}) copy-start(f32[256,512]{1,0:T(8,128)S(1)} %get-tuple-element.28) | copy-start | bytes 1572868
  126.9 1.5 copy-start.1
  128.1 4.3 %copy-start.15 = (f32[256,512]{1,0:T(8,128)}, f32[256,512]{1,0:T(8,128)S(1)}, u32[]{:S(2)}) copy-start(f32[256,512]{1,0:T(8,128)S(1)} %get-tuple-element.25) | copy-start | bytes 1572868
  128.1 4.3 %copy-start.17 = (f32[256,512]{1,0:T(8,128)}, f32[256,512]{1,0:T(8,128)S(1)}, u32[]{:S(2)}) copy-start(f32[256,512]{1,0:T(8,128)S(1)} %get-tuple-element.26) | copy-start | bytes 1572868
  132.0 3.6 %copy-start.5 = (f32[2,256,512]{2,1,0:T(8,128)}, f32[2,256,512]{2,1,0:T(8,128)S(1)}, u32[]{:S(2)}) copy-start(f32[2,256,512]{2,1,0:T(8,128)S(1)} %fusion.13) | copy-start | bytes 3145732
  147.1 4.7 %copy-start.3 = (f32[256,512]{1,0:T(8,128)S(1)}, f32[256,512]{1,0:T(8,128)}, u32[]{:S(2)}) copy-start(f32[256,512]{1,0:T(8,128)} %copy-done.2) | copy-start | bytes 1572868
  147.1 4.7 %copy-start.4 = (f32[2,256,512]{2,1,0:T(8,128)S(1)}, f32[2,256,512]{2,1,0:T(8,128)}, u32[]{:S(2)}) copy-start(f32[2,256,512]{2,1,0:T(8,128)} %get-tuple-element.24) | copy-start | bytes 3145732
  147.1 4.7 %copy-start.6 = (f32[2,256,512]{2,1,0:T(8,128)S(1)}, f32[2,256,512]{2,1,0:T(8,128)}, u32[]{:S(2)}) copy-start(f32[2,256,512]{2,1,0:T(8,128)} %get-tuple-element.8) | copy-start | bytes 3145732
  147.1 4.7 %copy-start.8 = (f32[256,512]{1,0:T(8,128)S(1)}, f32[256,512]{1,0:T(8,128)}, u32[]{:S(2)}) copy-start(f32[256,512]{1,0:T(8,128)} %copy-done.7) | copy-start | bytes 1572868
  147.1 4.7 %copy-start.10 = (f32[256,512]{1,0:T(8,128)S(1)}, f32[256,512]{1,0:T(8,128)}, u32[]{:S(2)}) copy-start(f32[256,512]{1,0:T(8,128)} %copy-done.9) | copy-start | bytes 1572868
  147.2 4.7 %copy-start.12 = (f32[256,512]{1,0:T(8,128)S(1)}, f32[256,512]{1,0:T(8,128)}, u32[]{:S(2)}) copy-start(f32[256,512]{1,0:T(8,128)} %copy-done.11) | copy-start | bytes 1572868
  147.2 4.7 %copy-start.14 = (f32[256,512]{1,0:T(8,128)S(1)}, f32[256,512]{1,0:T(8,128)}, u32[]{:S(2)}) copy-start(f32[256,512]{1,0:T(8,128)} %copy-done.13) | copy-start | bytes 1572868
  147.2 4.7 %copy-start.16 = (f32[256,512]{1,0:T(8,128)S(1)}, f32[256,512]{1,0:T(8,128)}, u32[]{:S(2)}) copy-start(f32[256,512]{1,0:T(8,128)} %copy-done.15) | copy-start | bytes 1572868
  147.2 4.7 %copy-start.18 = (f32[256,512]{1,0:T(8,128)S(1)}, f32[256,512]{1,0:T(8,128)}, u32[]{:S(2)}) copy-start(f32[256,512]{1,0:T(8,128)} %copy-done.17) | copy-start | bytes 1572868
  147.2 4.8 %copy-start.19 = (f32[2,256,512]{2,1,0:T(8,128)S(1)}, f32[2,256,512]{2,1,0:T(8,128)}, u32[]{:S(2)}) copy-start(f32[2,256,512]{2,1,0:T(8,128)} %get-tuple-element.5) | copy-start | bytes 3145732
  156.9 20.5 %copy-start.22 = (f32[2,128,512]{2,1,0:T(8,128)S(1)}, f32[2,128,512]{2,1,0:T(8,128)}, u32[]{:S(2)}) copy-start(f32[2,128,512]{2,1,0:T(8,128)} %param.9) | copy-start | bytes 1572868
Sparse Core Ops, SparseCore 0:
  10.1 55.8 all-gather.6
  68.7 54.1 all-gather.4
  157.1 20.2 all-reduce.21
where the time goes:
time: 187 us; the launch traced here: 186 us
  waiting for transfers between devices  130 us (70%)
  other arithmetic  36.4 us (19%)
  between operations  13.5 us (7%)
  local copies, waits for them, and re-layouts  5.07 us (3%)
    all_gather x2, waiting for transfers between devices, on_device(): stored = lax.all_gather(checkpoints[member], 'probe', axis=1, tiled=True)  109 us
    psum x1, waiting for transfers between devices, on_device(): summed = lax.psum(accumulated, 'shot')  20.2 us
    mul x4, other arithmetic, hessian_term(): coefficient * upcoming  19.3 us
    add x1, other arithmetic, on_device(): accumulated + hessian_term(vectors, levels, coefficient, weight_square)  4.94 us
    add x3, other arithmetic, on_device(): 2.0 * current - before + coefficient * laplace(current)  3.89 us
  transfers between devices with their start and end apart: 3, of which 3 were waited for; matrix products, arithmetic and copies ran while one was open for 3% of the time, Pallas kernels for 0%

commit v1 on v0

v1 whole, which is shorter than its diff:
```python
import functools

import jax
import jax.numpy as jnp
from jax import lax
from jax.experimental import pallas as pl
from jax.experimental.pallas import tpu as pltpu
from jax.sharding import PartitionSpec as P

MESH = pl.DeviceIdType.MESH
SUB = 8
LANE = 128
INNER = 4


def kernel(
    num_shot_devices,
    num_probe_devices,
    bounds_ref,
    encodings_ref,
    wavelet_ref,
    probes_hbm,
    coarse_hbm,
    coefficient_hbm,
    receiver_hbm,
    checkpoints_hbm,
    out_ref,
    gathered,
    probes_in,
    coarse_in,
    coefficient_in,
    receiver_in,
    coef,
    centre,
    weight,
    vec,
    um,
    u0,
    u1,
    u2,
    u3,
    d1,
    d2,
    d3,
    e4,
    e3,
    e2,
    total,
    flat,
    partial,
    inverse,
    parity_out,
    source,
    load_sem,
    own_sem,
    recv_sem,
    send_sem,
    swap_send,
    swap_recv,
):
    members, _, chunk, width = checkpoints_hbm.shape
    num_probes, num_rows, _ = probes_hbm.shape
    out_rows = coarse_hbm.shape[1]
    tiles = num_rows // SUB
    cols = [pl.ds(c * LANE, LANE) for c in range(width // LANE)]
    steps = wavelet_ref.shape[0]
    line = num_probe_devices // INNER
    flags = num_probe_devices * 2

    shot = lax.axis_index("shot")
    mine = lax.axis_index("probe")
    z = mine // INNER
    a = mine % INNER
    high, low = a // 2, a % 2
    right = 2 * low + (1 - high)
    left = 2 * (1 - low) + high

    places = {"a": a, "right": right, "left": left, "far": 3 - a}
    ids = {
        (dz, name): (z + dz) * INNER + place
        for dz in range(1 - line, line)
        for name, place in places.items()
    }
    toward = {1: z < line - 1, -1: z > 0}
    exists = {dz: (z + dz >= 0) & (z + dz < line) for dz in range(1 - line, line)}
    passes = {
        (dz, sign): exists[dz] & toward[sign] for dz in range(1 - line, line) for sign in (1, -1)
    }

    def slot(m, src, t):
        first = pl.multiple_of((src * 2 + t) * chunk, chunk)
        return gathered.at[m, :, pl.ds(first, chunk), :]

    def own_copy(m, t):
        first = pl.multiple_of((mine * 2 + t) * chunk, chunk)
        return [
            pltpu.make_async_copy(
                checkpoints_hbm.at[m, t, :, c],
                gathered.at[m, i, pl.ds(first, chunk), :],
                own_sem.at[(m * 2 + t) * len(cols) + i],
            )
            for i, c in enumerate(cols)
        ]

    for m in range(members):
        for t in range(2):
            for copy in own_copy(m, t):
                copy.start()

    count = len(cols)
    load_probes = [
        pltpu.make_async_copy(probes_hbm.at[:, :, c], probes_in.at[:, i], load_sem.at[i])
        for i, c in enumerate(cols)
    ]
    load_coefficient = [
        pltpu.make_async_copy(coefficient_hbm.at[:, c], coefficient_in.at[i], load_sem.at[count + i])
        for i, c in enumerate(cols)
    ]
    load_receiver = [
        pltpu.make_async_copy(receiver_hbm.at[:, c], receiver_in.at[i], load_sem.at[2 * count + i])
        for i, c in enumerate(cols)
    ]
    load_coarse = [pltpu.make_async_copy(coarse_hbm, coarse_in, load_sem.at[3 * count])]
    for load in load_coefficient + load_receiver + load_probes + load_coarse:
        load.start()

    barrier = pltpu.get_barrier_semaphore()

    def greet(device):
        pl.semaphore_signal(barrier, inc=1, device_id=device, device_id_type=MESH)

    greet({"probe": ids[0, "right"]})
    greet({"probe": ids[0, "left"]})

    @pl.when(z > 0)
    def _():
        greet({"probe": ids[-1, "a"]})

    @pl.when(z < line - 1)
    def _():
        greet({"probe": ids[1, "a"]})

    for away in range(1, num_shot_devices):
        greet({"shot": (shot + away) % num_shot_devices})
    inside = jnp.where(z > 0, 1, 0) + jnp.where(z < line - 1, 1, 0)
    pl.semaphore_wait(barrier, inside + 2 + num_shot_devices - 1)

    sent = []

    def send(m, src, t, target, lane, cond=None):
        def copy():
            return pltpu.make_async_remote_copy(
                src_ref=slot(m, ids[src], t),
                dst_ref=slot(m, ids[src], t),
                send_sem=send_sem.at[(lane * members + m) * flags + ids[src] * 2 + t],
                recv_sem=recv_sem.at[m * flags + ids[src] * 2 + t],
                device_id={"probe": ids[target]},
                device_id_type=MESH,
            )

        copy().start()
        sent.append((copy, cond))

    def arrive(m, src, t):
        pltpu.make_async_remote_copy(
            src_ref=slot(m, ids[src], t),
            dst_ref=slot(m, ids[src], t),
            send_sem=send_sem.at[m * flags + ids[src] * 2 + t],
            recv_sem=recv_sem.at[m * flags + ids[src] * 2 + t],
            device_id={"probe": ids[0, "right"]},
            device_id_type=MESH,
        ).wait_recv()

    def spread(m, src, cond=None):
        for t in (0, 1):
            send(m, src, t, (0, "right"), 2, cond)
            send(m, src, 1 - t, (0, "left"), 3, cond)

    def column(m, k):
        if k == 0:
            for t in range(2):
                for copy in own_copy(m, t):
                    copy.wait()
            for sign, lane in ((1, 0), (-1, 1)):

                @pl.when(toward[sign])
                def _(sign=sign, lane=lane):
                    for t in (0, 1):
                        send(m, (0, "a"), t, (sign, "a"), lane, toward[sign])

            spread(m, (0, "a"))
            return
        for sign, lane in ((1, 0), (-1, 1)):
            src = (-sign * k, "a")
            here = exists[-sign * k]
            more = passes[-sign * k, sign]

            @pl.when(here)
            def _(src=src):
                for t in (0, 1):
                    arrive(m, src, t)

            @pl.when(more)
            def _(src=src, sign=sign, lane=lane, more=more):
                for t in (0, 1):
                    send(m, src, t, (sign, "a"), lane, more)

            @pl.when(here)
            def _(src=src, here=here):
                spread(m, src, here)

    def sides(k):
        if k == 0:
            return ((0, None),)
        return ((-k, exists[-k]), (k, exists[k]))

    def guarded(cond, fun):
        if cond is None:
            fun()
        else:
            pl.when(cond)(fun)

    def relay(m, k):
        for dz, cond in sides(k):

            def run(dz=dz, cond=cond):
                arrive(m, (dz, "left"), 0)
                send(m, (dz, "left"), 0, (0, "right"), 2, cond)
                arrive(m, (dz, "right"), 1)
                send(m, (dz, "right"), 1, (0, "left"), 3, cond)

            guarded(cond, run)

    def finish(m, k):
        for dz, cond in sides(k):

            def run(dz=dz):
                arrive(m, (dz, "left"), 1)
                arrive(m, (dz, "right"), 0)
                arrive(m, (dz, "far"), 0)
                arrive(m, (dz, "far"), 1)

            guarded(cond, run)

    def gather_steps(m):
        plan = [lambda: column(m, 0)]
        for k in range(1, line):
            plan.append(lambda k=k: column(m, k))
            plan.append(lambda k=k: relay(m, k - 1))
        plan.append(lambda: relay(m, line - 1))
        return plan

    def gather_end(m):
        for k in range(line):
            finish(m, k)

    first_plan = gather_steps(0)
    first_plan[0]()

    row_in_tile = lax.broadcasted_iota(jnp.int32, (SUB, LANE), 0)
    lane_index = lax.broadcasted_iota(jnp.int32, (SUB, LANE), 1)
    at_first = lane_index == 0
    at_last = lane_index == LANE - 1

    def parity_of(rows):
        count = jnp.zeros((SUB, LANE), jnp.int32)
        for b in range(1, bounds_ref.shape[0] - 1):
            count = count + jnp.where(rows >= bounds_ref[b], 1, 0)
        return count % 2

    def prepare_sources():
        shots = wavelet_ref.shape[1]
        spacing = width // shots
        k = lax.broadcasted_iota(jnp.int32, (shots, width), 0)
        position = k * width // shots + spacing // 2
        column_index = lax.broadcasted_iota(jnp.int32, (shots, width), 1)
        onehot = jnp.where(position == column_index, 1.0, 0.0)
        for m in range(members):
            amplitude = encodings_ref[m : m + 1, :].astype(jnp.float32) * wavelet_ref[...]
            source[m, 0:steps, :] = jnp.dot(
                amplitude,
                onehot,
                precision=lax.Precision.HIGHEST,
                preferred_element_type=jnp.float32,
            )

    def strided(j):
        return pl.ds(j, SUB, stride=tiles)

    def prepare_fields():
        def body(j, carry):
            parity = parity_of(row_in_tile * tiles + j)
            for i, c in enumerate(cols):
                value = coefficient_in[i, strided(j), :]
                seen = receiver_in[i, strided(j), :]
                coef[j, :, c] = value
                centre[j, :, c] = 2.0 - 4.0 * value
                weight[j, :, c] = value * (seen * seen)
                for p in range(num_probes):
                    vec[p, j, :, c] = jnp.where(
                        parity == p % 2, probes_in[p, i, strided(j), :], 0.0
                    )
            return carry

        lax.fori_loop(0, tiles, body, 0)

    def prepare_out():
        def body(i, carry):
            first = shot * out_rows + i * SUB
            parity_out[i] = parity_of(row_in_tile + first)
            for n, c in enumerate(cols):
                rows = pl.ds(pl.multiple_of(first, SUB), SUB)
                inverse[i, :, c] = 1.0 / coefficient_in[n, rows, :]
            return carry

        lax.fori_loop(0, out_rows // SUB, body, 0)

    def halo(field):
        for c in cols:
            above = pltpu.roll(field[tiles, :, c], 1, 0)
            field[0, :, c] = jnp.where(row_in_tile == 0, 0.0, above)
            below = pltpu.roll(field[1, :, c], SUB - 1, 0)
            field[tiles + 1, :, c] = jnp.where(row_in_tile == SUB - 1, 0.0, below)

    def around(field, j):
        here = [field[j + 1, :, c] for c in cols]
        fore = [pltpu.roll(x, 1, 1) for x in here]
        back = [pltpu.roll(x, LANE - 1, 1) for x in here]
        near = []
        for i, c in enumerate(cols):
            west = jnp.where(at_first, fore[i - 1] if i else 0.0, fore[i])
            east = jnp.where(at_last, back[i + 1] if i + 1 < len(cols) else 0.0, back[i])
            near.append((field[j, :, c] + field[j + 2, :, c]) + (west + east))
        return here, near

    def advance(field, before, j):
        here, near = around(field, j)
        moved = []
        for i, c in enumerate(cols):
            value = centre[j, :, c] * here[i] + coef[j, :, c] * near[i]
            if before is not None:
                value = value - before(j, c)
            moved.append(value)
        return moved

    def inner(field):
        return lambda j, c: field[j + 1, :, c]

    def convert(m):
        per = tiles // chunk
        for block in range(per):

            def body(r, carry, block=block):
                j = block * chunk + r
                for i, c in enumerate(cols):
                    um[j, :, c] = gathered[
                        m, i, pl.ds((block * 2) * chunk + r, SUB, stride=2 * tiles), :
                    ]
                    value = gathered[
                        m, i, pl.ds((block * 2 + 1) * chunk + r, SUB, stride=2 * tiles), :
                    ]
                    u0[j + 1, :, c] = value
                    for p in range(num_probes):
                        d1[p, j + 1, :, c] = vec[p, j, :, c] * value
                return carry

            lax.fori_loop(0, chunk, body, 0)
        halo(u0)
        for p in range(num_probes):
            halo(d1.at[p])

    def forward(m, t):
        field = (u0, u1, u2)[t]
        before = (lambda j, c: um[j, :, c], inner(u0), inner(u1))[t]
        result = (u1, u2, u3)[t]
        delta = (d1, d2, d3)[t]
        delta_before = (None, d1, d2)[t]
        delta_next = (d2, d3, e4)[t]

        def body(j, first):
            moved = advance(field, before, j)
            if first:
                for i, c in enumerate(cols):
                    row = jnp.broadcast_to(source[m, t : t + 1, c], (SUB, LANE))
                    moved[i] = moved[i] + jnp.where(row_in_tile == SUB // 2, row, 0.0)
            for i, c in enumerate(cols):
                result[j + 1, :, c] = moved[i]
            for p in range(num_probes):
                prior = None if delta_before is None else inner(delta_before.at[p])
                step = advance(delta.at[p], prior, j)
                for i, c in enumerate(cols):
                    value = step[i] + vec[p, j, :, c] * moved[i]
                    if t < 2:
                        delta_next[p, j + 1, :, c] = value
                    else:
                        value = weight[j, :, c] * value
                        delta_next[p, j + 1, :, c] = value
                        gain = moved[i] * value
                        if m:
                            gain = total[p, j, :, c] + gain
                        total[p, j, :, c] = gain

        body(0, True)

        def rest(j, carry):
            body(j, False)
            return carry

        lax.fori_loop(1, tiles, rest, 0)
        if t < 2:
            halo(result)
        for p in range(num_probes):
            halo(delta_next.at[p])

    def adjoint(m, t, which):
        field = (e4, e3, e2)[t]
        before = (None, e4, e3)[t]
        result = (e3, e2, None)[t]
        delta = (d3, d2, d1)[t]
        level = (u2, u1, u0)[t]

        def body(j, carry):
            for p in which:
                prior = None if before is None else inner(before.at[p])
                step = advance(field.at[p], prior, j)
                for i, c in enumerate(cols):
                    value = step[i] + weight[j, :, c] * delta[p, j + 1, :, c]
                    if result is not None:
                        result[p, j + 1, :, c] = value
                    gain = total[p, j, :, c] + level[j + 1, :, c] * value
                    if result is None and m == members - 1:
                        flat[p, i, strided(j), :] = gain
                    else:
                        total[p, j, :, c] = gain
            return carry

        lax.fori_loop(0, tiles, body, 0)
        if result is not None:
            for p in which:
                halo(result.at[p])

    def swap(p):
        copies = []
        for away in range(1, num_shot_devices):
            other = (shot + away) % num_shot_devices
            copies.append(
                pltpu.make_async_remote_copy(
                    src_ref=flat.at[p, :, pl.ds(pl.multiple_of(other * out_rows, SUB), out_rows), :],
                    dst_ref=partial.at[away - 1, p],
                    send_sem=swap_send.at[away - 1, p],
                    recv_sem=swap_recv.at[away - 1, p],
                    device_id={"shot": other},
                    device_id_type=MESH,
                )
            )
        return copies

    def combine(p):
        def body(i, carry):
            first = pl.multiple_of(shot * out_rows + i * SUB, SUB)
            local = pl.ds(pl.multiple_of(i * SUB, SUB), SUB)
            keep = parity_out[i] != p % 2
            for n, c in enumerate(cols):
                value = flat[p, n, pl.ds(first, SUB), :]
                for away in range(1, num_shot_devices):
                    value = value + partial[away - 1, p, n, local, :]
                value = value * inverse[i, :, c] - coarse_in[p, local, c]
                out_ref[p, local, c] = jnp.where(keep, value, 0.0)
            return carry

        lax.fori_loop(0, out_rows // SUB, body, 0)

    everything = tuple(range(num_probes))
    prepare_sources()
    for load in load_coefficient:
        load.wait()
    first_plan[1]()
    first_plan[2]()
    prepare_out()
    first_plan[3]()
    for load in load_probes + load_receiver:
        load.wait()
    prepare_fields()
    for step in first_plan[4:]:
        step()
    load_coarse[0].wait()
    copies = [None] * num_probes
    for m in range(members):
        plan = gather_steps(m + 1) if m + 1 < members else []
        if plan:
            plan.pop(0)()
        gather_end(m)
        stages = [lambda: convert(m)]
        stages += [lambda t=t: forward(m, t) for t in range(3)]
        stages += [lambda t=t: adjoint(m, t, everything) for t in range(2)]
        if m < members - 1:
            stages.append(lambda: adjoint(m, 2, everything))
        for stage in stages:
            stage()
            if plan:
                plan.pop(0)()
        for step in plan:
            step()
    for p in everything:
        adjoint(members - 1, 2, (p,))
        copies[p] = swap(p)
        for copy in copies[p]:
            copy.start()
    for p in everything:
        for copy in copies[p]:
            copy.wait_recv()
        combine(p)
    for p in everything:
        for copy in copies[p]:
            copy.wait_send()
    for copy, cond in sent:
        guarded(cond, lambda copy=copy: copy().wait_send())


def on_device(
    num_shot_devices,
    num_probe_devices,
    probes,
    coarse_sample,
    coefficient,
    receiver,
    checkpoints,
    encodings,
    wavelet,
    bounds,
):
    members, levels, chunk, width = checkpoints.shape
    num_probes, num_rows, _ = probes.shape
    out_rows = coarse_sample.shape[1]
    tiles = num_rows // SUB
    groups = width // LANE
    f32 = jnp.float32

    def plain(*lead):
        return pltpu.VMEM((*lead, tiles, SUB, width), f32)

    def ringed(*lead):
        return pltpu.VMEM((*lead, tiles + 2, SUB, width), f32)

    others = num_shot_devices - 1
    anywhere = pl.BlockSpec(memory_space=pl.ANY)
    vmem = pl.BlockSpec(memory_space=pltpu.VMEM)
    return pl.pallas_call(
        functools.partial(kernel, num_shot_devices, num_probe_devices),
        out_shape=jax.ShapeDtypeStruct(coarse_sample.shape, f32),
        in_specs=[pl.BlockSpec(memory_space=pltpu.SMEM), vmem, vmem] + [anywhere] * 5,
        out_specs=vmem,
        scratch_shapes=[
            pltpu.VMEM((members, groups, levels * num_rows, LANE), f32),
            pltpu.VMEM((num_probes, groups, num_rows, LANE), f32),
            pltpu.VMEM(coarse_sample.shape, f32),
            pltpu.VMEM((groups, num_rows, LANE), f32),
            pltpu.VMEM((groups, num_rows, LANE), f32),
            plain(),
            plain(),
            plain(),
            plain(num_probes),
            plain(),
            ringed(),
            ringed(),
            ringed(),
            ringed(),
            ringed(num_probes),
            ringed(num_probes),
            ringed(num_probes),
            ringed(num_probes),
            ringed(num_probes),
            ringed(num_probes),
            plain(num_probes),
            pltpu.VMEM((num_probes, groups, num_rows, LANE), f32),
            pltpu.VMEM((others, num_probes, groups, out_rows, LANE), f32),
            pltpu.VMEM((out_rows // SUB, SUB, width), f32),
            pltpu.VMEM((out_rows // SUB, SUB, LANE), jnp.int32),
            pltpu.VMEM((members, SUB, width), f32),
            pltpu.SemaphoreType.DMA((3 * groups + 1,)),
            pltpu.SemaphoreType.DMA((members * levels * groups,)),
            pltpu.SemaphoreType.DMA((members * num_probe_devices * levels,)),
            pltpu.SemaphoreType.DMA((4 * members * num_probe_devices * levels,)),
            pltpu.SemaphoreType.DMA((others, num_probes)),
            pltpu.SemaphoreType.DMA((others, num_probes)),
        ],
        compiler_params=pltpu.CompilerParams(
            collective_id=0, has_side_effects=True, vmem_limit_bytes=60 * 1024 * 1024
        ),
    )(
        bounds,
        encodings,
        wavelet,
        probes,
        coarse_sample,
        coefficient,
        receiver,
        checkpoints,
    )


def solution(mesh):
    return jax.shard_map(
        functools.partial(on_device, mesh.shape["shot"], mesh.shape["probe"]),
        mesh=mesh,
        in_specs=(
            P("probe", None, None),
            P("probe", "shot", None),
            P(),
            P(),
            P("shot", None, "probe", None),
            P("shot", None),
            P(),
            P(),
        ),
        out_specs=P("probe", "shot", None),
        check_vma=False,
    )
```

time: 187 us -> 75.7 us (0.40)
  waiting for transfers between devices: 130 us -> 0 us
  Pallas kernels: 0 us -> 73.6 us
  other arithmetic: 36.4 us -> 0 us
  between operations: 13.5 us -> 0.01 us
  local copies, waits for them, and re-layouts: 5.07 us -> 1.87 us
    all_gather x2 -> x0, waiting for transfers between devices: 109 us -> none  [on_device(): stored = lax.all_gather(checkpoints[member], 'probe', axis=1, tiled=True)]
    pallas_call x0 -> x1, Pallas kernels: none -> 73.6 us  [on_device(): pl.pallas_call(functools.partial(kernel, num_shot_devices, num_probe_devi...]
    mul x6 -> x0, other arithmetic: 22.7 us -> none  [the longest x4 19.3 us: hessian_term(): coefficient * upcoming]
    psum x1 -> x0, waiting for transfers between devices: 20.2 us -> none  [on_device(): summed = lax.psum(accumulated, 'shot')]
    add x10 -> x0, other arithmetic: 12.3 us -> none  [the longest x1 4.94 us: on_device(): accumulated + hessian_term(vectors, levels, coefficient, weight_square)]
    slice x3 -> x0, local copies, waits for them, and re-layouts: 2.27 us -> none  [the longest x1 1.52 us: on_device(): stored = lax.all_gather(checkpoints[member], 'probe', axis=1, tiled=True)]
    squeeze x2 -> x0, local copies, waits for them, and re-layouts: 2.24 us -> none  [on_device(): current = stored[1]]
  transfers between devices with their start and end apart: 3 -> 0, of which waited for: 3 -> 0; matrix products, arithmetic and copies ran while one was open for 3% -> 0% of each run, Pallas kernels for 0% -> 0%
where the time goes in v1:
time: 75.7 us; the launch traced here: 75.5 us
  Pallas kernels  73.6 us (97%)
  local copies, waits for them, and re-layouts  1.87 us (2%)
    pallas_call x1, Pallas kernels, on_device(): pl.pallas_call(functools.partial(kernel, num_shot_devices, num_probe_devi...  73.6 us
    unnamed x1, local copies, waits for them, and re-layouts  1.87 us

profile of v1, /device:TPU:1, one launch (start us, length us, event | category | flops | bytes accessed | tf_op | source)
XLA Modules:
  0.0 75.5 jit_solution(16298707548873187188)
XLA Ops:
  0.0 73.6 %shard_map.82 = f32[2,128,512]{2,1,0:T(8,128)} custom-call(s32[33]{0:T(128)} %bounds_ref.1, s32[2,256]{1,0:T(2,128)} %encodings_ref.1, f32[3,256]{1,0:T(4,128)} %wavelet_ref.1, f32[2,256,512]{2,1,0:T(8,128)} %probes_hbm.1, f32[2,128,512]{2,1,0:T(8,128)} %coarse_hbm.1, f32[256,512]{1,0:T(8,128)} %coefficient_hbm.1, f32[256,512]{1,0:T(8,128)} %receiver_hbm.1, ...), custom_call_target="tpu_custom_call" | custom-call | tf_op jit(solution)/shard_map/pallas_call | solution.py:548
  73.7 1.9 %copy.10 = f32[2,128,512]{2,1,0:T(8,128)} copy(f32[2,128,512]{2,1,0:T(8,128)} %shard_map.82) | data formatting | bytes 1048576

commit v2 on v1

--- a/solution.py
+++ b/solution.py
@@ -55,6 +55,7 @@
     own_sem,
     recv_sem,
     send_sem,
+    line_sem,
     swap_send,
     swap_recv,
 ):
@@ -81,12 +82,7 @@
         for dz in range(1 - line, line)
         for name, place in places.items()
     }
-    toward = {1: z < line - 1, -1: z > 0}
     exists = {dz: (z + dz >= 0) & (z + dz < line) for dz in range(1 - line, line)}
-    passes = {
-        (dz, sign): exists[dz] & toward[sign] for dz in range(1 - line, line) for sign in (1, -1)
-    }
-
     def slot(m, src, t):
         first = pl.multiple_of((src * 2 + t) * chunk, chunk)
         return gathered.at[m, :, pl.ds(first, chunk), :]
@@ -132,27 +128,25 @@
     greet({"probe": ids[0, "right"]})
     greet({"probe": ids[0, "left"]})
 
-    @pl.when(z > 0)
-    def _():
-        greet({"probe": ids[-1, "a"]})
-
-    @pl.when(z < line - 1)
-    def _():
-        greet({"probe": ids[1, "a"]})
+    for dz in range(1 - line, line):
+        if dz:
+
+            @pl.when(exists[dz])
+            def _(dz=dz):
+                greet({"probe": ids[dz, "a"]})
 
     for away in range(1, num_shot_devices):
         greet({"shot": (shot + away) % num_shot_devices})
-    inside = jnp.where(z > 0, 1, 0) + jnp.where(z < line - 1, 1, 0)
-    pl.semaphore_wait(barrier, inside + 2 + num_shot_devices - 1)
+    pl.semaphore_wait(barrier, line - 1 + 2 + num_shot_devices - 1)
 
     sent = []
 
-    def send(m, src, t, target, lane, cond=None):
+    def send(m, src, t, target, sem, cond=None):
         def copy():
             return pltpu.make_async_remote_copy(
                 src_ref=slot(m, ids[src], t),
                 dst_ref=slot(m, ids[src], t),
-                send_sem=send_sem.at[(lane * members + m) * flags + ids[src] * 2 + t],
+                send_sem=sem(),
                 recv_sem=recv_sem.at[m * flags + ids[src] * 2 + t],
                 device_id={"probe": ids[target]},
                 device_id_type=MESH,
@@ -171,43 +165,45 @@
             device_id_type=MESH,
         ).wait_recv()
 
+    def ring(m, src, t, name, cond=None):
+        lane = 0 if name == "right" else 1
+        send(
+            m,
+            src,
+            t,
+            (0, name),
+            lambda: send_sem.at[(lane * members + m) * flags + ids[src] * 2 + t],
+            cond,
+        )
+
     def spread(m, src, cond=None):
         for t in (0, 1):
-            send(m, src, t, (0, "right"), 2, cond)
-            send(m, src, 1 - t, (0, "left"), 3, cond)
+            ring(m, src, t, "right", cond)
+            ring(m, src, 1 - t, "left", cond)
+
+    def begin(m):
+        for t in range(2):
+            for copy in own_copy(m, t):
+                copy.wait()
+        for k in range(1, line):
+            for dz in (k, -k):
+
+                @pl.when(exists[dz])
+                def _(dz=dz):
+                    for t in (0, 1):
+                        index = ((dz + line - 1) * members + m) * 2 + t
+                        send(m, (0, "a"), t, (dz, "a"), lambda index=index: line_sem.at[index], exists[dz])
+
+        spread(m, (0, "a"))
 
     def column(m, k):
-        if k == 0:
-            for t in range(2):
-                for copy in own_copy(m, t):
-                    copy.wait()
-            for sign, lane in ((1, 0), (-1, 1)):
-
-                @pl.when(toward[sign])
-                def _(sign=sign, lane=lane):
-                    for t in (0, 1):
-                        send(m, (0, "a"), t, (sign, "a"), lane, toward[sign])
-
-            spread(m, (0, "a"))
-            return
-        for sign, lane in ((1, 0), (-1, 1)):
-            src = (-sign * k, "a")
-            here = exists[-sign * k]
-            more = passes[-sign * k, sign]
+        for dz, here in sides(k):
 
             @pl.when(here)
-            def _(src=src):
+            def _(dz=dz, here=here):
                 for t in (0, 1):
-                    arrive(m, src, t)
-
-            @pl.when(more)
-            def _(src=src, sign=sign, lane=lane, more=more):
-                for t in (0, 1):
-                    send(m, src, t, (sign, "a"), lane, more)
-
-            @pl.when(here)
-            def _(src=src, here=here):
-                spread(m, src, here)
+                    arrive(m, (dz, "a"), t)
+                spread(m, (dz, "a"), here)
 
     def sides(k):
         if k == 0:
@@ -225,9 +221,9 @@
 
             def run(dz=dz, cond=cond):
                 arrive(m, (dz, "left"), 0)
-                send(m, (dz, "left"), 0, (0, "right"), 2, cond)
+                ring(m, (dz, "left"), 0, "right", cond)
                 arrive(m, (dz, "right"), 1)
-                send(m, (dz, "right"), 1, (0, "left"), 3, cond)
+                ring(m, (dz, "right"), 1, "left", cond)
 
             guarded(cond, run)
 
@@ -243,7 +239,7 @@
             guarded(cond, run)
 
     def gather_steps(m):
-        plan = [lambda: column(m, 0)]
+        plan = []
         for k in range(1, line):
             plan.append(lambda k=k: column(m, k))
             plan.append(lambda k=k: relay(m, k - 1))
@@ -254,8 +250,8 @@
         for k in range(line):
             finish(m, k)
 
-    first_plan = gather_steps(0)
-    first_plan[0]()
+    for m in range(members):
+        begin(m)
 
     row_in_tile = lax.broadcasted_iota(jnp.int32, (SUB, LANE), 0)
     lane_index = lax.broadcasted_iota(jnp.int32, (SUB, LANE), 1)
@@ -287,7 +283,7 @@
     def strided(j):
         return pl.ds(j, SUB, stride=tiles)
 
-    def prepare_fields():
+    def prepare_fields(first, last):
         def body(j, carry):
             parity = parity_of(row_in_tile * tiles + j)
             for i, c in enumerate(cols):
@@ -302,7 +298,7 @@
                     )
             return carry
 
-        lax.fori_loop(0, tiles, body, 0)
+        lax.fori_loop(first, last, body, 0, unroll=2)
 
     def prepare_out():
         def body(i, carry):
@@ -313,7 +309,7 @@
                 inverse[i, :, c] = 1.0 / coefficient_in[n, rows, :]
             return carry
 
-        lax.fori_loop(0, out_rows // SUB, body, 0)
+        lax.fori_loop(0, out_rows // SUB, body, 0, unroll=2)
 
     def halo(field):
         for c in cols:
@@ -364,7 +360,7 @@
                         d1[p, j + 1, :, c] = vec[p, j, :, c] * value
                 return carry
 
-            lax.fori_loop(0, chunk, body, 0)
+            lax.fori_loop(0, chunk, body, 0, unroll=2)
         halo(u0)
         for p in range(num_probes):
             halo(d1.at[p])
@@ -406,7 +402,7 @@
             body(j, False)
             return carry
 
-        lax.fori_loop(1, tiles, rest, 0)
+        lax.fori_loop(1, tiles, rest, 0, unroll=4)
         if t < 2:
             halo(result)
         for p in range(num_probes):
@@ -434,7 +430,7 @@
                         total[p, j, :, c] = gain
             return carry
 
-        lax.fori_loop(0, tiles, body, 0)
+        lax.fori_loop(0, tiles, body, 0, unroll=4)
         if result is not None:
             for p in which:
                 halo(result.at[p])
@@ -472,22 +468,24 @@
 
     everything = tuple(range(num_probes))
     prepare_sources()
-    for load in load_coefficient:
+    for load in load_coefficient + load_receiver + load_probes:
         load.wait()
-    first_plan[1]()
-    first_plan[2]()
-    prepare_out()
-    first_plan[3]()
-    for load in load_probes + load_receiver:
-        load.wait()
-    prepare_fields()
-    for step in first_plan[4:]:
+    work = []
+    for q in range(4):
+        work.append(lambda q=q: prepare_fields(q * tiles // 4, (q + 1) * tiles // 4))
+    work.append(prepare_out)
+    for step in gather_steps(0):
         step()
+        if work:
+            work.pop(0)()
+    for rest in work:
+        rest()
     load_coarse[0].wait()
     copies = [None] * num_probes
     for m in range(members):
         plan = gather_steps(m + 1) if m + 1 < members else []
         if plan:
+            plan.pop(0)()
             plan.pop(0)()
         gather_end(m)
         stages = [lambda: convert(m)]
@@ -534,6 +532,7 @@
     out_rows = coarse_sample.shape[1]
     tiles = num_rows // SUB
     groups = width // LANE
+    line = num_probe_devices // INNER
     f32 = jnp.float32
 
     def plain(*lead):
@@ -580,7 +579,8 @@
             pltpu.SemaphoreType.DMA((3 * groups + 1,)),
             pltpu.SemaphoreType.DMA((members * levels * groups,)),
             pltpu.SemaphoreType.DMA((members * num_probe_devices * levels,)),
-            pltpu.SemaphoreType.DMA((4 * members * num_probe_devices * levels,)),
+            pltpu.SemaphoreType.DMA((2 * members * num_probe_devices * levels,)),
+            pltpu.SemaphoreType.DMA(((2 * line - 1) * members * levels,)),
             pltpu.SemaphoreType.DMA((others, num_probes)),
             pltpu.SemaphoreType.DMA((others, num_probes)),
         ],

time: 75.7 us -> 52 us (0.69)
  Pallas kernels: 73.6 us -> 50 us
    pallas_call x1, Pallas kernels: 73.6 us -> 50 us  [on_device(): pl.pallas_call(functools.partial(kernel, num_shot_devices, num_probe_devi...]
where the time goes in v2:
time: 52 us; the launch traced here: 51.9 us
  Pallas kernels  50 us (96%)
  local copies, waits for them, and re-layouts  1.87 us (4%)
    pallas_call x1, Pallas kernels, on_device(): pl.pallas_call(functools.partial(kernel, num_shot_devices, num_probe_devi...  50 us
    unnamed x1, local copies, waits for them, and re-layouts  1.87 us

profile of v2, /device:TPU:1, one launch (start us, length us, event | category | flops | bytes accessed | tf_op | source)
XLA Modules:
  0.0 51.9 jit_solution(7720257912446442885)
XLA Ops:
  0.0 50.0 %shard_map.82 = f32[2,128,512]{2,1,0:T(8,128)} custom-call(s32[33]{0:T(128)} %bounds_ref.1, s32[2,256]{1,0:T(2,128)} %encodings_ref.1, f32[3,256]{1,0:T(4,128)} %wavelet_ref.1, f32[2,256,512]{2,1,0:T(8,128)} %probes_hbm.1, f32[2,128,512]{2,1,0:T(8,128)} %coarse_hbm.1, f32[256,512]{1,0:T(8,128)} %coefficient_hbm.1, f32[256,512]{1,0:T(8,128)} %receiver_hbm.1, ...), custom_call_target="tpu_custom_call" | custom-call | tf_op jit(solution)/shard_map/pallas_call | solution.py:547
  50.0 1.9 %copy.10 = f32[2,128,512]{2,1,0:T(8,128)} copy(f32[2,128,512]{2,1,0:T(8,128)} %shard_map.82) | data formatting | bytes 1048576

commit v3 on v2

--- a/solution.py
+++ b/solution.py
@@ -242,8 +242,8 @@
         plan = []
         for k in range(1, line):
             plan.append(lambda k=k: column(m, k))
-            plan.append(lambda k=k: relay(m, k - 1))
-        plan.append(lambda: relay(m, line - 1))
+        for k in range(line):
+            plan.append(lambda k=k: relay(m, k))
         return plan
 
     def gather_end(m):
@@ -485,8 +485,8 @@
     for m in range(members):
         plan = gather_steps(m + 1) if m + 1 < members else []
         if plan:
-            plan.pop(0)()
-            plan.pop(0)()
+            for _ in range(line - 1):
+                plan.pop(0)()
         gather_end(m)
         stages = [lambda: convert(m)]
         stages += [lambda t=t: forward(m, t) for t in range(3)]

time: 52 us -> 51.2 us (0.985)
  Pallas kernels: 50 us -> 49.1 us
    pallas_call x1, Pallas kernels: 50 us -> 49.1 us  [on_device(): pl.pallas_call(functools.partial(kernel, num_shot_devices, num_probe_devi...]
where the time goes in v3:
time: 51.2 us; the launch traced here: 51 us
  Pallas kernels  49.1 us (96%)
  local copies, waits for them, and re-layouts  1.87 us (4%)
    pallas_call x1, Pallas kernels, on_device(): pl.pallas_call(functools.partial(kernel, num_shot_devices, num_probe_devi...  49.1 us
    unnamed x1, local copies, waits for them, and re-layouts  1.87 us

profile of v3, /device:TPU:1, one launch (start us, length us, event | category | flops | bytes accessed | tf_op | source)
XLA Modules:
  0.0 51.0 jit_solution(14718634163924049558)
XLA Ops:
  0.0 49.1 %shard_map.82 = f32[2,128,512]{2,1,0:T(8,128)} custom-call(s32[33]{0:T(128)} %bounds_ref.1, s32[2,256]{1,0:T(2,128)} %encodings_ref.1, f32[3,256]{1,0:T(4,128)} %wavelet_ref.1, f32[2,256,512]{2,1,0:T(8,128)} %probes_hbm.1, f32[2,128,512]{2,1,0:T(8,128)} %coarse_hbm.1, f32[256,512]{1,0:T(8,128)} %coefficient_hbm.1, f32[256,512]{1,0:T(8,128)} %receiver_hbm.1, ...), custom_call_target="tpu_custom_call" | custom-call | tf_op jit(solution)/shard_map/pallas_call | solution.py:547
  49.1 1.9 %copy.10 = f32[2,128,512]{2,1,0:T(8,128)} copy(f32[2,128,512]{2,1,0:T(8,128)} %shard_map.82) | data formatting | bytes 1048576
